TPU v7x, 32 devices: a whole 2x2x4 slice. The times are simulated.
32 devices in a mesh: mesh: 8 (over y, x, core), band: 4 (over z).
Axes of the slice: x: 2, y: 2, z: 4, core: 2. Of those that a mesh axis runs over, the one named last changes fastest.
Arguments:
- states: float32 [2, 64, 8192], P(None, 'band', 'mesh'), may hold values from -6 to 6
- frozen: float32 [2, 32, 8192], P(None, 'band', 'mesh'), may hold values from -0.125 to 0.125
- weights: float32 [8, 8192], P(None, 'mesh'), may hold values from 0.1 to 1
- potential: float32 [8192], P('mesh'), may hold values from -2 to 2
- send_list: int32 [8, 8, 256], P('mesh'), may hold values from 0 to 1023
- neighbours: int32 [8, 8192], P(None, 'mesh'), may hold values from 0 to 3071, as said below
Outputs:
- evolved: float32 [2, 64, 8192], P(None, 'band', 'mesh')
Inputs may be any that keep to these rules, and one draw needn't show every extreme that they name: `neighbours`: an entry below 1024 names a point of the same part; an entry 1024 + s * 256 + c names ghost slot c from part s, where part s is at most 3 parts away in the cyclic order of parts or exactly half the number of parts away, and every part names ghost slots from all those parts. Slots of send_list[s, i] that part i never names hold arbitrary points of part s.
All inputs are finite; a program needn't handle non-finite values.
Results may differ from a plain program's by a relative error of at most 0.0001.
Values sent between devices are 32-bit elements; how exact they have to be, the bound alone decides.
No kernel may reach another device: no remote copies, remote signals or barrier semaphores. Data moves between devices by JAX's collectives and lax.ppermute only.
A program may use at most 128 MiB of HBM per device.

v0:
```python
import jax
import jax.numpy as jnp
from jax import lax
from jax.sharding import PartitionSpec as P

NBRS = 8
TERMS = 4
time_step = 0.3


def rotate(field):
    return jnp.stack([field[1], -field[0]])


def body(states, frozen, weights, potential, send_list, neighbours):
    parts = lax.axis_size("mesh")
    rows = states.shape[1]
    capacity = send_list.shape[2]
    routes = send_list[0]
    full_frozen = lax.all_gather(frozen, "band", axis=1, tiled=True)
    total = states
    term = states
    for order in range(1, TERMS + 1):
        paired = jnp.stack([term, rotate(term)])
        partial_intersection = jnp.einsum(
            "cmp,ocjp->omj", full_frozen, paired, precision=lax.Precision.HIGHEST
        )
        intersection = lax.psum(partial_intersection, "mesh")
        packed = jnp.take(term, routes.reshape(-1), axis=2).reshape(2, rows, parts, capacity)
        arrived = lax.all_to_all(packed, "mesh", split_axis=2, concat_axis=2, tiled=True)
        extended = jnp.concatenate([term, arrived.reshape(2, rows, parts * capacity)], axis=2)
        stencil = jnp.zeros_like(term)
        for apply_order in range(NBRS):
            stencil = stencil + weights[apply_order] * (
                jnp.take(extended, neighbours[apply_order], axis=2) - term
            )
        blocks = jnp.stack(
            [
                jnp.stack([intersection[0], -intersection[1]]),
                jnp.stack([intersection[1], intersection[0]]),
            ]
        )
        exchange = jnp.einsum("dmp,cdmj->cjp", full_frozen, blocks, precision=lax.Precision.HIGHEST)
        image = -0.5 * stencil + potential * term - exchange
        term = time_step / order * rotate(image)
        total = total + term
    return total


def solution(mesh):
    return jax.shard_map(
        body,
        mesh=mesh,
        in_specs=(
            P(None, "band", "mesh"),
            P(None, "band", "mesh"),
            P(None, "mesh"),
            P("mesh"),
            P("mesh", None, None),
            P(None, "mesh"),
        ),
        out_specs=P(None, "band", "mesh"),
        check_vma=False,
    )
```

profile of v0, /device:TPU:0, one launch (start us, length us, event | category | flops | bytes accessed | tf_op | source)
XLA Modules:
  0.0 581.9 jit_solution(13586005560089532101)
XLA Ops:
  2.1 14.4 %gather_fusion = f32[2048,2,16]{2,1,0:T(2,128)} fusion(f32[2,16,1024]{1,0,2:T(2,128)S(1)} %copy.119, s32[2048]{0:T(1024)S(1)} %fusion.108), kind=kCustom, calls=%fused_computation.clone | custom fusion | bytes 532480 | tf_op jit(solution)/shard_map/jit(_take)/gather | solution.py:29
  16.5 10.0 %broadcast_select_fusion.3 = f32[2048,2,16]{2,1,0:T(2,128)S(1)} fusion(f32[2048,2,16]{2,1,0:T(2,128)} %gather_fusion, pred[2048]{0:T(1024)(128)(4,1)S(1)} %compare_and_fusion), kind=kLoop, calls=%fused_computation.39 | loop fusion | flops 65536 | bytes 526336 | tf_op jit(solution)/shard_map/jit(_take)/select_n | solution.py:29
  39.6 14.2 %all_gather.3 = f32[2,32,1024]{2,1,0:T(8,128)S(1)} all-gather(f32[2,8,1024]{2,1,0:T(8,128)S(1)} %copy-done.34), channel_id=1, replica_groups=mesh['mesh'=8,'band'=4] {'band'}, dimensions={1}, use_global_device_ids=true | all-gather | bytes 327680 | tf_op jit(solution)/shard_map/all_gather | solution.py:20
  54.3 23.0 %psum.28 = f32[2,32,16]{1,2,0:T(8,128)S(1)} all-reduce(f32[2,32,16]{1,2,0:T(8,128)S(1)} %convolution_bitcast_fusion.7), channel_id=1, replica_groups=mesh['mesh'=8,'band'=4] {'mesh'}, use_global_device_ids=true, to_apply=%region_0.3 | all-reduce | flops 1024 | bytes 8192 | tf_op jit(solution)/shard_map/psum | solution.py:28
  84.0 7.6 %gather_fusion.1 = f32[1024,2,16]{2,1,0:T(2,128)} fusion(f32[2,16,3072]{1,0,2:T(2,128)S(1)} %copy.122, s32[1024]{0:T(1024)} %fusion.109), kind=kCustom, calls=%fused_computation.1.clone | custom fusion | bytes 266240 | tf_op jit(solution)/shard_map/jit(_take)/gather | solution.py:35
  112.9 7.6 %gather_fusion.4 = f32[1024,2,16]{2,1,0:T(2,128)} fusion(f32[2,16,3072]{1,0,2:T(2,128)S(1)} %copy.122, s32[1024]{0:T(1024)} %fusion.112), kind=kCustom, calls=%fused_computation.7.clone | custom fusion | bytes 266240 | tf_op jit(solution)/shard_map/jit(_take)/gather | solution.py:35
  132.1 7.6 %gather_fusion.6 = f32[1024,2,16]{2,1,0:T(2,128)} fusion(f32[2,16,3072]{1,0,2:T(2,128)S(1)} %copy.122, s32[1024]{0:T(1024)} %fusion.114), kind=kCustom, calls=%fused_computation.9.clone | custom fusion | bytes 266240 | tf_op jit(solution)/shard_map/jit(_take)/gather | solution.py:35
  163.5 22.3 %psum.29 = f32[2,32,16]{1,2,0:T(8,128)S(1)} all-reduce(f32[2,32,16]{1,2,0:T(8,128)S(1)} %convolution_bitcast_fusion.6), channel_id=1, replica_groups=mesh['mesh'=8,'band'=4] {'mesh'}, use_global_device_ids=true, to_apply=%region_1.4 | all-reduce | flops 1024 | bytes 8192 | tf_op jit(solution)/shard_map/psum | solution.py:28
  185.8 14.4 %gather_fusion.9 = f32[2048,2,16]{2,1,0:T(2,128)} fusion(f32[2,16,1024]{1,0,2:T(2,128)S(1)} %copy.138, s32[2048]{0:T(1024)S(1)} %fusion.108), kind=kCustom, calls=%fused_computation.2.clone | custom fusion | bytes 532480 | tf_op jit(solution)/shard_map/jit(_take)/gather | solution.py:29
  200.2 10.0 %broadcast_select_fusion.2 = f32[2048,2,16]{2,1,0:T(2,128)S(1)} fusion(f32[2048,2,16]{2,1,0:T(2,128)} %gather_fusion.9, pred[2048]{0:T(1024)(128)(4,1)S(1)} %copy-done.36), kind=kLoop, calls=%fused_computation.38 | loop fusion | flops 65536 | bytes 526336 | tf_op jit(solution)/shard_map/jit(_take)/select_n | solution.py:29
  227.3 7.6 %gather_fusion.10 = f32[1024,2,16]{2,1,0:T(2,128)} fusion(f32[2,16,3072]{1,0,2:T(2,128)S(1)} %copy.141, s32[1024]{0:T(1024)} %fusion.109), kind=kCustom, calls=%fused_computation.12.clone | custom fusion | bytes 266240 | tf_op jit(solution)/shard_map/jit(_take)/gather | solution.py:35
  235.0 7.6 %gather_fusion.11 = f32[1024,2,16]{2,1,0:T(2,128)} fusion(f32[2,16,3072]{1,0,2:T(2,128)S(1)} %copy.141, s32[1024]{0:T(1024)} %fusion.110), kind=kCustom, calls=%fused_computation.13.clone | custom fusion | bytes 266240 | tf_op jit(solution)/shard_map/jit(_take)/gather | solution.py:35
  242.6 7.6 %gather_fusion.12 = f32[1024,2,16]{2,1,0:T(2,128)} fusion(f32[2,16,3072]{1,0,2:T(2,128)S(1)} %copy.141, s32[1024]{0:T(1024)} %fusion.111), kind=kCustom, calls=%fused_computation.14.clone | custom fusion | bytes 266240 | tf_op jit(solution)/shard_map/jit(_take)/gather | solution.py:35
  250.2 7.6 %gather_fusion.13 = f32[1024,2,16]{2,1,0:T(2,128)} fusion(f32[2,16,3072]{1,0,2:T(2,128)S(1)} %copy.141, s32[1024]{0:T(1024)} %fusion.112), kind=kCustom, calls=%fused_computation.15.clone | custom fusion | bytes 266240 | tf_op jit(solution)/shard_map/jit(_take)/gather | solution.py:35
  303.7 22.3 %psum.30 = f32[2,32,16]{1,2,0:T(8,128)S(1)} all-reduce(f32[2,32,16]{1,2,0:T(8,128)S(1)} %convolution_bitcast_fusion.5), channel_id=1, replica_groups=mesh['mesh'=8,'band'=4] {'mesh'}, use_global_device_ids=true, to_apply=%region_2.5 | all-reduce | flops 1024 | bytes 8192 | tf_op jit(solution)/shard_map/psum | solution.py:28
  326.0 14.4 %gather_fusion.18 = f32[2048,2,16]{2,1,0:T(2,128)} fusion(f32[2,16,1024]{1,0,2:T(2,128)S(1)} %copy.157, s32[2048]{0:T(1024)S(1)} %fusion.108), kind=kCustom, calls=%fused_computation.3.clone | custom fusion | bytes 532480 | tf_op jit(solution)/shard_map/jit(_take)/gather | solution.py:29
  340.4 10.0 %broadcast_select_fusion.1 = f32[2048,2,16]{2,1,0:T(2,128)S(1)} fusion(f32[2048,2,16]{2,1,0:T(2,128)} %gather_fusion.18, pred[2048]{0:T(1024)(128)(4,1)S(1)} %copy-done.37), kind=kLoop, calls=%fused_computation.37 | loop fusion | flops 65536 | bytes 526336 | tf_op jit(solution)/shard_map/jit(_take)/select_n | solution.py:29
  367.5 7.6 %gather_fusion.19 = f32[1024,2,16]{2,1,0:T(2,128)} fusion(f32[2,16,3072]{1,0,2:T(2,128)S(1)} %copy.160, s32[1024]{0:T(1024)} %fusion.109), kind=kCustom, calls=%fused_computation.20.clone | custom fusion | bytes 266240 | tf_op jit(solution)/shard_map/jit(_take)/gather | solution.py:35
  375.2 7.6 %gather_fusion.20 = f32[1024,2,16]{2,1,0:T(2,128)} fusion(f32[2,16,3072]{1,0,2:T(2,128)S(1)} %copy.160, s32[1024]{0:T(1024)} %fusion.110), kind=kCustom, calls=%fused_computation.21.clone | custom fusion | bytes 266240 | tf_op jit(solution)/shard_map/jit(_take)/gather | solution.py:35
  382.8 7.6 %gather_fusion.21 = f32[1024,2,16]{2,1,0:T(2,128)} fusion(f32[2,16,3072]{1,0,2:T(2,128)S(1)} %copy.160, s32[1024]{0:T(1024)} %fusion.111), kind=kCustom, calls=%fused_computation.22.clone | custom fusion | bytes 266240 | tf_op jit(solution)/shard_map/jit(_take)/gather | solution.py:35
  390.4 7.6 %gather_fusion.22 = f32[1024,2,16]{2,1,0:T(2,128)} fusion(f32[2,16,3072]{1,0,2:T(2,128)S(1)} %copy.160, s32[1024]{0:T(1024)} %fusion.112), kind=kCustom, calls=%fused_computation.23.clone | custom fusion | bytes 266240 | tf_op jit(solution)/shard_map/jit(_take)/gather | solution.py:35
  443.8 22.3 %psum.31 = f32[2,32,16]{1,2,0:T(8,128)S(1)} all-reduce(f32[2,32,16]{1,2,0:T(8,128)S(1)} %convolution_bitcast_fusion.4), channel_id=1, replica_groups=mesh['mesh'=8,'band'=4] {'mesh'}, use_global_device_ids=true, to_apply=%region_3.6 | all-reduce | flops 1024 | bytes 8192 | tf_op jit(solution)/shard_map/psum | solution.py:28
  466.1 14.4 %gather_fusion.27 = f32[2048,2,16]{2,1,0:T(2,128)} fusion(f32[2,16,1024]{1,0,2:T(2,128)S(1)} %copy.176, s32[2048]{0:T(1024)S(1)} %fusion.108), kind=kCustom, calls=%fused_computation.4.clone | custom fusion | bytes 532480 | tf_op jit(solution)/shard_map/jit(_take)/gather | solution.py:29
  480.6 10.0 %broadcast_select_fusion = f32[2048,2,16]{2,1,0:T(2,128)S(1)} fusion(f32[2048,2,16]{2,1,0:T(2,128)} %gather_fusion.27, pred[2048]{0:T(1024)(128)(4,1)S(1)} %copy-done.38), kind=kLoop, calls=%fused_computation.36 | loop fusion | flops 65536 | bytes 526336 | tf_op jit(solution)/shard_map/jit(_take)/select_n | solution.py:29
  (218 shorter events, 295.4 us)
Async XLA Ops:
  0.7 27.7 %copy-start.35 = (pred[2048]{0:T(1024)(128)(4,1)}, pred[2048]{0:T(1024)(128)(4,1)S(1)}, u32[]{:S(2)}) copy-start(pred[2048]{0:T(1024)(128)(4,1)S(1)} %compare_and_fusion) | copy-start | bytes 6148
  16.5 17.1 %copy-start = (f32[2,16,1024]{2,1,0:T(8,128)S(1)}, f32[2,16,1024]{2,1,0:T(8,128)}, u32[]{:S(2)}) copy-start(f32[2,16,1024]{2,1,0:T(8,128)} %param.10) | copy-start | bytes 393220
  16.5 17.1 %copy-start.39 = (s32[8,1024]{1,0:T(8,128)S(1)}, s32[8,1024]{1,0:T(8,128)}, u32[]{:S(2)}) copy-start(s32[8,1024]{1,0:T(8,128)} %param.15) | copy-start | bytes 98308
  16.5 23.1 %copy-start.34 = (f32[2,8,1024]{2,1,0:T(8,128)S(1)}, f32[2,8,1024]{2,1,0:T(8,128)}, u32[]{:S(2)}) copy-start(f32[2,8,1024]{2,1,0:T(8,128)} %param.11) | copy-start | bytes 196612
  26.5 50.7 %copy-start.41 = (f32[1024]{0:T(1024)S(1)}, f32[1024]{0:T(1024)}, u32[]{:S(2)}) copy-start(f32[1024]{0:T(1024)} %param.13) | copy-start | bytes 12292
  26.6 51.9 %copy-start.40 = (f32[8,1024]{1,0:T(8,128)S(1)}, f32[8,1024]{1,0:T(8,128)}, u32[]{:S(2)}) copy-start(f32[8,1024]{1,0:T(8,128)} %param.12) | copy-start | bytes 98308
  28.5 50.6 %all-to-all-start = ((f32[2,16,8,256]{3,1,0,2:T(8,128)}), f32[2,16,8,256]{3,1,0,2:T(8,128)S(1)}, u32[]{:S(2)}, u32[]{:S(2)}) async-start(f32[2,16,8,256]{3,1,0,2:T(8,128)} %copy.120), calls=%async_computation | async-start | bytes 524288 | tf_op jit(solution)/shard_map/all_to_all | solution.py:30
  158.7 41.6 %copy-start.36 = (pred[2048]{0:T(1024)(128)(4,1)S(1)}, pred[2048]{0:T(1024)(128)(4,1)}, u32[]{:S(2)}) copy-start(pred[2048]{0:T(1024)(128)(4,1)} %copy-done.35) | copy-start | bytes 6148
  212.1 10.3 %all-to-all-start.1 = ((f32[2,16,8,256]{3,1,0,2:T(8,128)}), f32[2,16,8,256]{3,1,0,2:T(8,128)S(1)}, u32[]{:S(2)}, u32[]{:S(2)}) async-start(f32[2,16,8,256]{3,1,0,2:T(8,128)} %copy.139), calls=%async_computation.1 | async-start | bytes 524288 | tf_op jit(solution)/shard_map/all_to_all | solution.py:30
  287.9 10.4 %copy-start.9 = (f32[1024,2,16]{2,1,0:T(2,128)S(1)}, f32[1024,2,16]{2,1,0:T(2,128)}, u32[]{:S(2)}) copy-start(f32[1024,2,16]{2,1,0:T(2,128)} %gather_fusion.15) | copy-start | bytes 393220
  290.0 9.3 %copy-start.7 = (f32[1024,2,16]{2,1,0:T(2,128)S(1)}, f32[1024,2,16]{2,1,0:T(2,128)}, u32[]{:S(2)}) copy-start(f32[1024,2,16]{2,1,0:T(2,128)} %gather_fusion.16) | copy-start | bytes 393220
  292.2 7.6 %copy-start.5 = (f32[1024,2,16]{2,1,0:T(2,128)S(1)}, f32[1024,2,16]{2,1,0:T(2,128)}, u32[]{:S(2)}) copy-start(f32[1024,2,16]{2,1,0:T(2,128)} %gather_fusion.17) | copy-start | bytes 393220
  299.8 40.6 %copy-start.37 = (pred[2048]{0:T(1024)(128)(4,1)S(1)}, pred[2048]{0:T(1024)(128)(4,1)}, u32[]{:S(2)}) copy-start(pred[2048]{0:T(1024)(128)(4,1)} %copy-done.35) | copy-start | bytes 6148
  352.3 10.3 %all-to-all-start.2 = ((f32[2,16,8,256]{3,1,0,2:T(8,128)}), f32[2,16,8,256]{3,1,0,2:T(8,128)S(1)}, u32[]{:S(2)}, u32[]{:S(2)}) async-start(f32[2,16,8,256]{3,1,0,2:T(8,128)} %copy.158), calls=%async_computation.2 | async-start | bytes 524288 | tf_op jit(solution)/shard_map/all_to_all | solution.py:30
  428.1 10.4 %copy-start.10 = (f32[1024,2,16]{2,1,0:T(2,128)S(1)}, f32[1024,2,16]{2,1,0:T(2,128)}, u32[]{:S(2)}) copy-start(f32[1024,2,16]{2,1,0:T(2,128)} %gather_fusion.24) | copy-start | bytes 393220
  430.2 9.3 %copy-start.8 = (f32[1024,2,16]{2,1,0:T(2,128)S(1)}, f32[1024,2,16]{2,1,0:T(2,128)}, u32[]{:S(2)}) copy-start(f32[1024,2,16]{2,1,0:T(2,128)} %gather_fusion.25) | copy-start | bytes 393220
  432.4 7.6 %copy-start.6 = (f32[1024,2,16]{2,1,0:T(2,128)S(1)}, f32[1024,2,16]{2,1,0:T(2,128)}, u32[]{:S(2)}) copy-start(f32[1024,2,16]{2,1,0:T(2,128)} %gather_fusion.26) | copy-start | bytes 393220
  440.0 40.6 %copy-start.38 = (pred[2048]{0:T(1024)(128)(4,1)S(1)}, pred[2048]{0:T(1024)(128)(4,1)}, u32[]{:S(2)}) copy-start(pred[2048]{0:T(1024)(128)(4,1)} %copy-done.35) | copy-start | bytes 6148
  492.4 45.7 %copy-start.29 = (s32[1024]{0:T(1024)S(1)}, s32[1024]{0:T(1024)}, u32[]{:S(2)}) copy-start(s32[1024]{0:T(1024)} %fusion.113) | copy-start | bytes 12292
  492.4 10.4 %all-to-all-start.3 = ((f32[2,16,8,256]{3,1,0,2:T(8,128)}), f32[2,16,8,256]{3,1,0,2:T(8,128)S(1)}, u32[]{:S(2)}, u32[]{:S(2)}) async-start(f32[2,16,8,256]{3,1,0,2:T(8,128)} %copy.177), calls=%async_computation.3 | async-start | bytes 524288 | tf_op jit(solution)/shard_map/all_to_all | solution.py:30
  496.2 49.5 %copy-start.28 = (s32[1024]{0:T(1024)S(1)}, s32[1024]{0:T(1024)}, u32[]{:S(2)}) copy-start(s32[1024]{0:T(1024)} %fusion.114) | copy-start | bytes 12292
  568.2 6.2 %copy-start.1 = (f32[1024,2,16]{2,1,0:T(2,128)S(1)}, f32[1024,2,16]{2,1,0:T(2,128)}, u32[]{:S(2)}) copy-start(f32[1024,2,16]{2,1,0:T(2,128)} %gather_fusion.31) | copy-start | bytes 393220
  568.2 7.3 %copy-start.2 = (f32[1024,2,16]{2,1,0:T(2,128)S(1)}, f32[1024,2,16]{2,1,0:T(2,128)}, u32[]{:S(2)}) copy-start(f32[1024,2,16]{2,1,0:T(2,128)} %gather_fusion.32) | copy-start | bytes 393220
  568.2 8.4 %copy-start.3 = (f32[1024,2,16]{2,1,0:T(2,128)S(1)}, f32[1024,2,16]{2,1,0:T(2,128)}, u32[]{:S(2)}) copy-start(f32[1024,2,16]{2,1,0:T(2,128)} %gather_fusion.33) | copy-start | bytes 393220
  (22 other events, 67.4 us)
where the time goes:
time: 585 us; the launch traced here: 582 us
  local copies, waits for them, and re-layouts  382 us (65%)
  blocking collectives  104 us (18%)
  other arithmetic  53 us (9%)
  waiting for transfers between devices  18.3 us (3%)
  starting transfers between devices  15.9 us (3%)
  matrix products  8.07 us (1%)
    gather x64, local copies, waits for them, and re-layouts, body(): jnp.take(extended, neighbours[apply_order], axis=2) - term  293 us
    psum x4, blocking collectives, body(): intersection = lax.psum(partial_intersection, 'mesh')  89.9 us
    gather x4, local copies, waits for them, and re-layouts, body(): jnp.take(term, routes.reshape(-1), axis=2).reshape(2, rows, parts, capacity)  57.7 us
    select_n x4, other arithmetic, body(): jnp.take(term, routes.reshape(-1), axis=2).reshape(2, rows, parts, capacity)  39.9 us
    all_to_all x4, waiting for transfers between devices, body(): lax.all_to_all(packed, 'mesh', split_axis=2, concat_axis=2, tiled=True)  18.3 us
    concatenate x4, local copies, waits for them, and re-layouts, body(): jnp.concatenate([term, arrived.reshape(2, rows, parts * capacity)], axis=2)  16.6 us
    all_to_all x4, starting transfers between devices, body(): lax.all_to_all(packed, 'mesh', split_axis=2, concat_axis=2, tiled=True)  15.9 us
    all_gather x1, blocking collectives, body(): full_frozen = lax.all_gather(frozen, 'band', axis=1, tiled=True)  14.2 us
  transfers between devices with their start and end apart: 4, of which 3 were waited for; matrix products, arithmetic and copies ran while one was open for 2% of the time, Pallas kernels for 0%

commit v1 on v0

--- a/solution.py
+++ b/solution.py
@@ -6,6 +6,18 @@
 NBRS = 8
 TERMS = 4
 time_step = 0.3
+
+
+def cut_along(x, dim, size):
+    dims = x.shape
+    blocks = x.reshape(*dims[:dim], size, dims[dim] // size, *dims[dim + 1 :])
+    return jnp.moveaxis(blocks, dim, 0)
+
+
+def laid_out(blocks, dim):
+    blocks = jnp.moveaxis(blocks, 0, dim)
+    dims = blocks.shape
+    return blocks.reshape(*dims[:dim], dims[dim] * dims[dim + 1], *dims[dim + 2 :])
 
 
 def rotate(field):
@@ -27,7 +39,14 @@
         )
         intersection = lax.psum(partial_intersection, "mesh")
         packed = jnp.take(term, routes.reshape(-1), axis=2).reshape(2, rows, parts, capacity)
-        arrived = lax.all_to_all(packed, "mesh", split_axis=2, concat_axis=2, tiled=True)
+        count, mine = (lax.axis_size("mesh"), lax.axis_index("mesh"))
+        pieces = cut_along(packed, 2, count)
+        done = [pieces[mine]]
+        for lap in range(1, count):
+            sent = pieces[mine ^ lap]
+            done.append(lax.ppermute(sent, "mesh", [(i, i ^ lap) for i in range(count)]))
+        pieces = jnp.stack(done)[mine ^ jnp.arange(count)]
+        arrived = laid_out(pieces, 2)
         extended = jnp.concatenate([term, arrived.reshape(2, rows, parts * capacity)], axis=2)
         stencil = jnp.zeros_like(term)
         for apply_order in range(NBRS):

time: 585 us -> 557 us (0.952)
  local copies, waits for them, and re-layouts: 382 us -> 360 us
  other arithmetic: 53 us -> 41.7 us
  starting transfers between devices: 15.9 us -> 24.8 us
  waiting for transfers between devices: 18.3 us -> 11.7 us
    gather x4, local copies, waits for them, and re-layouts: 57.7 us -> 30.9 us  [body(): jnp.take(term, routes.reshape(-1), axis=2).reshape(2, rows, parts, capacity)]
    ppermute x0 -> x28, starting transfers between devices: none -> 24.8 us  [body(): lax.ppermute(sent, 'mesh', [(i, i ^ lap) for i in range(count)])]
    all_to_all x4 -> x0, waiting for transfers between devices: 18.3 us -> none  [body(): lax.all_to_all(packed, 'mesh', split_axis=2, concat_axis=2, tiled=True)]
    all_to_all x4 -> x0, starting transfers between devices: 15.9 us -> none  [body(): lax.all_to_all(packed, 'mesh', split_axis=2, concat_axis=2, tiled=True)]
    ppermute x0 -> x28, waiting for transfers between devices: none -> 11.7 us  [body(): lax.ppermute(sent, 'mesh', [(i, i ^ lap) for i in range(count)])]
    select_n x4, other arithmetic: 39.9 us -> 29.8 us  [body(): jnp.take(term, routes.reshape(-1), axis=2).reshape(2, rows, parts, capacity)]
    reshape x8 -> x0, local copies, waits for them, and re-layouts: 7.63 us -> none  [the longest x4 7.56 us: body(): jnp.take(term, routes.reshape(-1), axis=2).reshape(2, rows, parts, capacity)]
  transfers between devices with their start and end apart: 4 -> 28, of which waited for: 3 -> 7; matrix products, arithmetic and copies ran while one was open for 2% -> 2% of each run, Pallas kernels for 0% -> 0%
where the time goes in v1:
time: 557 us; the launch traced here: 555 us
  local copies, waits for them, and re-layouts  360 us (65%)
  blocking collectives  108 us (19%)
  other arithmetic  41.7 us (7%)
  starting transfers between devices  24.8 us (4%)
  waiting for transfers between devices  11.7 us (2%)
  matrix products  8.06 us (1%)
    gather x64, local copies, waits for them, and re-layouts, body(): jnp.take(extended, neighbours[apply_order], axis=2) - term  296 us
    psum x4, blocking collectives, body(): intersection = lax.psum(partial_intersection, 'mesh')  93.2 us
    gather x4, local copies, waits for them, and re-layouts, body(): jnp.take(term, routes.reshape(-1), axis=2).reshape(2, rows, parts, capacity)  30.9 us
    select_n x4, other arithmetic, body(): jnp.take(term, routes.reshape(-1), axis=2).reshape(2, rows, parts, capacity)  29.8 us
    ppermute x28, starting transfers between devices, body(): lax.ppermute(sent, 'mesh', [(i, i ^ lap) for i in range(count)])  24.8 us
    concatenate x4, local copies, waits for them, and re-layouts, body(): jnp.concatenate([term, arrived.reshape(2, rows, parts * capacity)], axis=2)  16.6 us
    all_gather x1, blocking collectives, body(): full_frozen = lax.all_gather(frozen, 'band', axis=1, tiled=True)  14.4 us
    ppermute x28, waiting for transfers between devices, body(): lax.ppermute(sent, 'mesh', [(i, i ^ lap) for i in range(count)])  11.7 us
  transfers between devices with their start and end apart: 28, of which 7 were waited for; matrix products, arithmetic and copies ran while one was open for 2% of the time, Pallas kernels for 0%

profile of v1, /device:TPU:0, one launch (start us, length us, event | category | flops | bytes accessed | tf_op | source)
XLA Modules:
  0.0 554.9 jit_solution(10426989873664411568)
XLA Ops:
  27.1 14.4 %all_gather.3 = f32[2,32,1024]{2,1,0:T(8,128)S(1)} all-gather(f32[2,8,1024]{2,1,0:T(8,128)S(1)} %copy-done.32), channel_id=1, replica_groups=mesh['mesh'=8,'band'=4] {'band'}, dimensions={1}, use_global_device_ids=true | all-gather | bytes 327680 | tf_op jit(solution)/shard_map/all_gather | solution.py:32
  41.9 22.7 %psum.28 = f32[2,32,16]{1,2,0:T(8,128)S(1)} all-reduce(f32[2,32,16]{1,2,0:T(8,128)S(1)} %convolution_bitcast_fusion.7), channel_id=1, replica_groups=mesh['mesh'=8,'band'=4] {'mesh'}, use_global_device_ids=true, to_apply=%region_0.3 | all-reduce | flops 1024 | bytes 8192 | tf_op jit(solution)/shard_map/psum | solution.py:40
  77.3 7.7 %gather_fusion.5 = f32[1024,2,16]{2,1,0:T(2,128)} fusion(f32[2,16,3072]{1,0,2:T(2,128)S(1)} %copy.141, s32[1024]{0:T(1024)} %get-tuple-element.100), kind=kCustom, calls=%fused_computation.1.clone | custom fusion | bytes 266240 | tf_op jit(solution)/shard_map/jit(_take)/gather | solution.py:54
  96.6 7.7 %gather_fusion.7 = f32[1024,2,16]{2,1,0:T(2,128)} fusion(f32[2,16,3072]{1,0,2:T(2,128)S(1)} %copy.141, s32[1024]{0:T(1024)} %get-tuple-element.102), kind=kCustom, calls=%fused_computation.6.clone | custom fusion | bytes 266240 | tf_op jit(solution)/shard_map/jit(_take)/gather | solution.py:54
  106.3 7.7 %gather_fusion.8 = f32[1024,2,16]{2,1,0:T(2,128)} fusion(f32[2,16,3072]{1,0,2:T(2,128)S(1)} %copy.141, s32[1024]{0:T(1024)} %get-tuple-element.103), kind=kCustom, calls=%fused_computation.7.clone | custom fusion | bytes 266240 | tf_op jit(solution)/shard_map/jit(_take)/gather | solution.py:54
  125.7 7.7 %gather_fusion.10 = f32[1024,2,16]{2,1,0:T(2,128)} fusion(f32[2,16,3072]{1,0,2:T(2,128)S(1)} %copy.141, s32[1024]{0:T(1024)} %get-tuple-element.105), kind=kCustom, calls=%fused_computation.9.clone | custom fusion | bytes 266240 | tf_op jit(solution)/shard_map/jit(_take)/gather | solution.py:54
  135.4 7.7 %gather_fusion.11 = f32[1024,2,16]{2,1,0:T(2,128)} fusion(f32[2,16,3072]{1,0,2:T(2,128)S(1)} %copy.141, s32[1024]{0:T(1024)} %get-tuple-element.106), kind=kCustom, calls=%fused_computation.10.clone | custom fusion | bytes 266240 | tf_op jit(solution)/shard_map/jit(_take)/gather | solution.py:54
  145.0 7.7 %gather_fusion.12 = f32[1024,2,16]{2,1,0:T(2,128)} fusion(f32[2,16,3072]{1,0,2:T(2,128)S(1)} %copy.141, s32[1024]{0:T(1024)} %get-tuple-element.107), kind=kCustom, calls=%fused_computation.11.clone | custom fusion | bytes 266240 | tf_op jit(solution)/shard_map/jit(_take)/gather | solution.py:54
  158.2 22.5 %psum.29 = f32[2,32,16]{1,2,0:T(8,128)S(1)} all-reduce(f32[2,32,16]{1,2,0:T(8,128)S(1)} %convolution_bitcast_fusion.6), channel_id=1, replica_groups=mesh['mesh'=8,'band'=4] {'mesh'}, use_global_device_ids=true, to_apply=%region_1.4 | all-reduce | flops 1024 | bytes 8192 | tf_op jit(solution)/shard_map/psum | solution.py:40
  180.7 8.0 %gather_fusion.13 = f32[2048,2,16]{2,1,0:T(2,128)S(1)} fusion(f32[2,16,1024]{1,0,2:T(2,128)} %copy.157, s32[2048]{0:T(1024)S(1)} %fusion.108), kind=kCustom, calls=%fused_computation.2.clone | custom fusion | bytes 532480 | tf_op jit(solution)/shard_map/jit(_take)/gather | solution.py:41
  220.3 7.7 %gather_fusion.15 = f32[1024,2,16]{2,1,0:T(2,128)} fusion(f32[2,16,3072]{1,0,2:T(2,128)S(1)} %copy.167, s32[1024]{0:T(1024)} %get-tuple-element.101), kind=kCustom, calls=%fused_computation.13.clone | custom fusion | bytes 266240 | tf_op jit(solution)/shard_map/jit(_take)/gather | solution.py:54
  228.0 7.7 %gather_fusion.16 = f32[1024,2,16]{2,1,0:T(2,128)} fusion(f32[2,16,3072]{1,0,2:T(2,128)S(1)} %copy.167, s32[1024]{0:T(1024)} %get-tuple-element.102), kind=kCustom, calls=%fused_computation.14.clone | custom fusion | bytes 266240 | tf_op jit(solution)/shard_map/jit(_take)/gather | solution.py:54
  243.3 7.7 %gather_fusion.18 = f32[1024,2,16]{2,1,0:T(2,128)} fusion(f32[2,16,3072]{1,0,2:T(2,128)S(1)} %copy.167, s32[1024]{0:T(1024)} %get-tuple-element.104), kind=kCustom, calls=%fused_computation.16.clone | custom fusion | bytes 266240 | tf_op jit(solution)/shard_map/jit(_take)/gather | solution.py:54
  266.3 7.7 %gather_fusion.21 = f32[1024,2,16]{2,1,0:T(2,128)} fusion(f32[2,16,3072]{1,0,2:T(2,128)S(1)} %copy.167, s32[1024]{0:T(1024)} %get-tuple-element.107), kind=kCustom, calls=%fused_computation.19.clone | custom fusion | bytes 266240 | tf_op jit(solution)/shard_map/jit(_take)/gather | solution.py:54
  290.4 24.0 %psum.30 = f32[2,32,16]{1,2,0:T(8,128)S(1)} all-reduce(f32[2,32,16]{1,2,0:T(8,128)S(1)} %convolution_bitcast_fusion.5), channel_id=1, replica_groups=mesh['mesh'=8,'band'=4] {'mesh'}, use_global_device_ids=true, to_apply=%region_2.5 | all-reduce | flops 1024 | bytes 8192 | tf_op jit(solution)/shard_map/psum | solution.py:40
  314.4 8.0 %gather_fusion.22 = f32[2048,2,16]{2,1,0:T(2,128)S(1)} fusion(f32[2,16,1024]{1,0,2:T(2,128)} %copy.183, s32[2048]{0:T(1024)S(1)} %fusion.108), kind=kCustom, calls=%fused_computation.3.clone | custom fusion | bytes 532480 | tf_op jit(solution)/shard_map/jit(_take)/gather | solution.py:41
  354.1 7.7 %gather_fusion.24 = f32[1024,2,16]{2,1,0:T(2,128)} fusion(f32[2,16,3072]{1,0,2:T(2,128)S(1)} %copy.193, s32[1024]{0:T(1024)} %get-tuple-element.101), kind=kCustom, calls=%fused_computation.21.clone | custom fusion | bytes 266240 | tf_op jit(solution)/shard_map/jit(_take)/gather | solution.py:54
  361.8 7.7 %gather_fusion.25 = f32[1024,2,16]{2,1,0:T(2,128)} fusion(f32[2,16,3072]{1,0,2:T(2,128)S(1)} %copy.193, s32[1024]{0:T(1024)} %get-tuple-element.102), kind=kCustom, calls=%fused_computation.22.clone | custom fusion | bytes 266240 | tf_op jit(solution)/shard_map/jit(_take)/gather | solution.py:54
  377.1 7.7 %gather_fusion.27 = f32[1024,2,16]{2,1,0:T(2,128)} fusion(f32[2,16,3072]{1,0,2:T(2,128)S(1)} %copy.193, s32[1024]{0:T(1024)} %get-tuple-element.104), kind=kCustom, calls=%fused_computation.24.clone | custom fusion | bytes 266240 | tf_op jit(solution)/shard_map/jit(_take)/gather | solution.py:54
  400.1 7.7 %gather_fusion.30 = f32[1024,2,16]{2,1,0:T(2,128)} fusion(f32[2,16,3072]{1,0,2:T(2,128)S(1)} %copy.193, s32[1024]{0:T(1024)} %get-tuple-element.107), kind=kCustom, calls=%fused_computation.27.clone | custom fusion | bytes 266240 | tf_op jit(solution)/shard_map/jit(_take)/gather | solution.py:54
  424.2 24.0 %psum.31 = f32[2,32,16]{1,2,0:T(8,128)S(1)} all-reduce(f32[2,32,16]{1,2,0:T(8,128)S(1)} %convolution_bitcast_fusion.4), channel_id=1, replica_groups=mesh['mesh'=8,'band'=4] {'mesh'}, use_global_device_ids=true, to_apply=%region_3.6 | all-reduce | flops 1024 | bytes 8192 | tf_op jit(solution)/shard_map/psum | solution.py:40
  448.2 8.0 %gather_fusion.31 = f32[2048,2,16]{2,1,0:T(2,128)S(1)} fusion(f32[2,16,1024]{1,0,2:T(2,128)} %copy.209, s32[2048]{0:T(1024)S(1)} %fusion.108), kind=kCustom, calls=%fused_computation.4.clone | custom fusion | bytes 532480 | tf_op jit(solution)/shard_map/jit(_take)/gather | solution.py:41
  503.1 7.7 %gather_fusion.35 = f32[1024,2,16]{2,1,0:T(2,128)} fusion(f32[2,16,3072]{1,0,2:T(2,128)S(1)} %copy.219, s32[1024]{0:T(1024)} %get-tuple-element.103), kind=kCustom, calls=%fused_computation.31.clone | custom fusion | bytes 266240 | tf_op jit(solution)/shard_map/jit(_take)/gather | solution.py:54
  518.4 7.7 %gather_fusion.37 = f32[1024,2,16]{2,1,0:T(2,128)} fusion(f32[2,16,3072]{1,0,2:T(2,128)S(1)} %copy.219, s32[1024]{0:T(1024)} %get-tuple-element.105), kind=kCustom, calls=%fused_computation.33.clone | custom fusion | bytes 266240 | tf_op jit(solution)/shard_map/jit(_take)/gather | solution.py:54
  (334 shorter events, 299.2 us)
Async XLA Ops:
  16.8 49.9 %collective-permute-start = (f32[2,16,1,256]{3,1,0,2:T(8,128)S(1)}, f32[2,16,1,256]{3,1,0,2:T(8,128)S(1)}, u32[]{:S(2)}, u32[]{:S(2)}) collective-permute-start(f32[2,16,1,256]{3,1,0,2:T(8,128)S(1)} %bitcast.581), channel_id=1, source_target_pairs={{0,4},{4,0},{8,12},{12,8},{16,20},{20,16},{24,28},{28,24},{1,5},{5... | collective-permute-start | bytes 98312 | tf_op jit(solution)/shard_map/ppermute | solution.py:47
  17.4 49.4 %collective-permute-start.1 = (f32[2,16,1,256]{3,1,0,2:T(8,128)S(1)}, f32[2,16,1,256]{3,1,0,2:T(8,128)S(1)}, u32[]{:S(2)}, u32[]{:S(2)}) collective-permute-start(f32[2,16,1,256]{3,1,0,2:T(8,128)S(1)} %bitcast.580), channel_id=1, source_target_pairs={{0,8},{4,12},{8,0},{12,4},{16,24},{20,28},{24,16},{28,20},{1,9},{5... | collective-permute-start | bytes 98312 | tf_op jit(solution)/shard_map/ppermute | solution.py:47
  20.0 46.8 %collective-permute-start.2 = (f32[2,16,1,256]{3,1,0,2:T(8,128)S(1)}, f32[2,16,1,256]{3,1,0,2:T(8,128)S(1)}, u32[]{:S(2)}, u32[]{:S(2)}) collective-permute-start(f32[2,16,1,256]{3,1,0,2:T(8,128)S(1)} %bitcast.579), channel_id=1, source_target_pairs={{0,12},{4,8},{8,4},{12,0},{16,28},{20,24},{24,20},{28,16},{1,13},{... | collective-permute-start | bytes 98312 | tf_op jit(solution)/shard_map/ppermute | solution.py:47
  20.3 46.6 %collective-permute-start.3 = (f32[2,16,1,256]{3,1,0,2:T(8,128)S(1)}, f32[2,16,1,256]{3,1,0,2:T(8,128)S(1)}, u32[]{:S(2)}, u32[]{:S(2)}) collective-permute-start(f32[2,16,1,256]{3,1,0,2:T(8,128)S(1)} %bitcast.578), channel_id=1, source_target_pairs={{0,16},{4,20},{8,24},{12,28},{16,0},{20,4},{24,8},{28,12},{1,17},{... | collective-permute-start | bytes 98312 | tf_op jit(solution)/shard_map/ppermute | solution.py:47
  22.2 44.7 %collective-permute-start.4 = (f32[2,16,1,256]{3,1,0,2:T(8,128)S(1)}, f32[2,16,1,256]{3,1,0,2:T(8,128)S(1)}, u32[]{:S(2)}, u32[]{:S(2)}) collective-permute-start(f32[2,16,1,256]{3,1,0,2:T(8,128)S(1)} %bitcast.577), channel_id=1, source_target_pairs={{0,20},{4,16},{8,28},{12,24},{16,4},{20,0},{24,12},{28,8},{1,21},{... | collective-permute-start | bytes 98312 | tf_op jit(solution)/shard_map/ppermute | solution.py:47
  66.6 4.9 collective-permute-start.5
  66.7 4.8 collective-permute-start.6
  196.6 5.0 collective-permute-start.7
  196.8 5.6 %collective-permute-start.8 = (f32[2,16,1,256]{3,1,0,2:T(8,128)S(1)}, f32[2,16,1,256]{3,1,0,2:T(8,128)S(1)}, u32[]{:S(2)}, u32[]{:S(2)}) collective-permute-start(f32[2,16,1,256]{3,1,0,2:T(8,128)S(1)} %bitcast.599), channel_id=1, source_target_pairs={{0,8},{4,12},{8,0},{12,4},{16,24},{20,28},{24,16},{28,20},{1,9},{5... | collective-permute-start | bytes 98312 | tf_op jit(solution)/shard_map/ppermute | solution.py:47
  197.0 7.5 %collective-permute-start.9 = (f32[2,16,1,256]{3,1,0,2:T(8,128)S(1)}, f32[2,16,1,256]{3,1,0,2:T(8,128)S(1)}, u32[]{:S(2)}, u32[]{:S(2)}) collective-permute-start(f32[2,16,1,256]{3,1,0,2:T(8,128)S(1)} %bitcast.589), channel_id=1, source_target_pairs={{0,12},{4,8},{8,4},{12,0},{16,28},{20,24},{24,20},{28,16},{1,13},{... | collective-permute-start | bytes 98312 | tf_op jit(solution)/shard_map/ppermute | solution.py:47
  198.9 5.5 collective-permute-start.10
  201.6 5.0 collective-permute-start.12
  330.3 5.0 collective-permute-start.14
  330.5 5.6 %collective-permute-start.15 = (f32[2,16,1,256]{3,1,0,2:T(8,128)S(1)}, f32[2,16,1,256]{3,1,0,2:T(8,128)S(1)}, u32[]{:S(2)}, u32[]{:S(2)}) collective-permute-start(f32[2,16,1,256]{3,1,0,2:T(8,128)S(1)} %bitcast.600), channel_id=1, source_target_pairs={{0,8},{4,12},{8,0},{12,4},{16,24},{20,28},{24,16},{28,20},{1,9},{5... | collective-permute-start | bytes 98312 | tf_op jit(solution)/shard_map/ppermute | solution.py:47
  330.7 7.5 %collective-permute-start.16 = (f32[2,16,1,256]{3,1,0,2:T(8,128)S(1)}, f32[2,16,1,256]{3,1,0,2:T(8,128)S(1)}, u32[]{:S(2)}, u32[]{:S(2)}) collective-permute-start(f32[2,16,1,256]{3,1,0,2:T(8,128)S(1)} %bitcast.591), channel_id=1, source_target_pairs={{0,12},{4,8},{8,4},{12,0},{16,28},{20,24},{24,20},{28,16},{1,13},{... | collective-permute-start | bytes 98312 | tf_op jit(solution)/shard_map/ppermute | solution.py:47
  332.7 5.5 collective-permute-start.17
  335.3 5.0 collective-permute-start.19
  336.2 4.4 collective-permute-start.20
  464.1 5.0 collective-permute-start.21
  464.2 5.6 %collective-permute-start.22 = (f32[2,16,1,256]{3,1,0,2:T(8,128)S(1)}, f32[2,16,1,256]{3,1,0,2:T(8,128)S(1)}, u32[]{:S(2)}, u32[]{:S(2)}) collective-permute-start(f32[2,16,1,256]{3,1,0,2:T(8,128)S(1)} %bitcast.601), channel_id=1, source_target_pairs={{0,8},{4,12},{8,0},{12,4},{16,24},{20,28},{24,16},{28,20},{1,9},{5... | collective-permute-start | bytes 98312 | tf_op jit(solution)/shard_map/ppermute | solution.py:47
  464.4 7.5 %collective-permute-start.23 = (f32[2,16,1,256]{3,1,0,2:T(8,128)S(1)}, f32[2,16,1,256]{3,1,0,2:T(8,128)S(1)}, u32[]{:S(2)}, u32[]{:S(2)}) collective-permute-start(f32[2,16,1,256]{3,1,0,2:T(8,128)S(1)} %bitcast.593), channel_id=1, source_target_pairs={{0,12},{4,8},{8,4},{12,0},{16,28},{20,24},{24,20},{28,16},{1,13},{... | collective-permute-start | bytes 98312 | tf_op jit(solution)/shard_map/ppermute | solution.py:47
  466.4 5.5 collective-permute-start.24
  469.1 5.0 collective-permute-start.26
  469.9 4.4 collective-permute-start.27
  (45 other events, 502.4 us)
